TPU v7x, 256 devices: a whole 4x4x8 slice. The times are simulated.
256 devices in a mesh: space: 32 (over y_hi, z, core), coil: 8 (over y_lo, x).
Axes of the slice: x: 4, y: 4 (y_hi: 2, y_lo: 2; y = y_hi * 2 + y_lo), z: 8, core: 2. Of those that a mesh axis runs over, the one named last changes fastest.
Arguments:
- spatial_coef: bfloat16 [16, 128, 128, 2, 128], P('coil', 'space'), may hold values from -6 to 6
- temporal_basis: bfloat16 [2, 16, 4], replicated, may hold values from -1.5 to 1.5
- coil_maps: bfloat16 [32, 128, 128, 2, 128], P('coil', 'space'), may hold values from -6 to 6
- field_steps: int32 [128, 128, 128], P('space'), may hold values from 0 to 255
- kspace_data: bfloat16 [32, 4, 128, 128, 2, 128], P('coil', None, None, 'space'), may hold values from -6 to 6
- sample_mask: int32 [4, 128, 128], P(None, 'space'), may hold values 0 or 1
Outputs:
- gradient: float32 [16, 128, 128, 2, 128], P('coil', 'space')
Inputs may be any that keep to these rules, and one draw needn't show every extreme that they name: `sample_mask`: 1 where a phase-encoding line is sampled at that point, else 0.
All inputs are finite; a program needn't handle non-finite values. No bound on the sum of `sample_mask` on one device may be relied on, other than what follows from the above.
Results may differ from a plain program's by a relative error of at most 0.014.
Values may be sent and summed in bfloat16 or wider, within the bound.
A program may use at most 64 MiB of HBM per device.

v0:
```python
import math
import jax
import jax.numpy as jnp
from jax import lax
from jax.sharding import PartitionSpec as P

STEPS_CYCLE = 256


def dft_table(length, sign):
    index = jnp.arange(length, dtype=jnp.int32)
    steps = index[:, None] * index[None, :] % length
    angle = steps.astype(jnp.float32) * (2.0 * math.pi / length)
    scale = 1.0 / math.sqrt(length)
    cosine = jnp.cos(angle) * scale
    sine = jnp.sin(angle) * (sign * scale)
    upper = jnp.stack([cosine, sine], axis=1)
    lower = jnp.stack([-sine, cosine], axis=1)
    return jnp.stack([upper, lower], axis=0).astype(jnp.bfloat16)


def forward_mix(basis):
    real_part = basis[0]
    imaginary = basis[1]
    return jnp.stack(
        [jnp.stack([real_part, imaginary], -1), jnp.stack([-imaginary, real_part], -1)], 1
    )


def adjoint_mix(basis):
    real_part = basis[0].T
    imaginary = basis[1].T
    return jnp.stack(
        [jnp.stack([real_part, -imaginary], -1), jnp.stack([imaginary, real_part], -1)], 1
    )


def phase_parts(field_steps, points):
    counter = jnp.arange(1, points + 1, dtype=jnp.int32)
    steps = field_steps[None] * counter[:, None, None, None] % STEPS_CYCLE
    angle = steps.astype(jnp.float32) * (2.0 * math.pi / STEPS_CYCLE)
    return (jnp.cos(angle), jnp.sin(angle))


def transform(volume, table, form):
    return jnp.einsum(form, volume, table, preferred_element_type=jnp.float32)


def shards(spatial_coef, temporal_basis, coil_maps, field_steps, kspace_data, sample_mask):
    points = temporal_basis.shape[2]
    section = temporal_basis
    image = jnp.einsum(
        "lxypz,lptq->txyqz",
        lax.all_gather(spatial_coef, "coil", axis=0, tiled=True),
        forward_mix(section),
        preferred_element_type=jnp.float32,
    )
    cosine, sine = phase_parts(field_steps, points)
    image_real = image[:, :, :, 0]
    image_imaginary = image[:, :, :, 1]
    turned_real = cosine * image_real - sine * image_imaginary
    turned_imaginary = sine * image_real + cosine * image_imaginary
    map_real = coil_maps[:, :, :, 0].astype(jnp.float32)[:, None]
    map_imaginary = coil_maps[:, :, :, 1].astype(jnp.float32)[:, None]
    coil_real = map_real * turned_real - map_imaginary * turned_imaginary
    coil_imaginary = map_real * turned_imaginary + map_imaginary * turned_real
    coil_image = jnp.stack([coil_real, coil_imaginary], axis=4).astype(jnp.bfloat16)
    depth_count = coil_image.shape[5]
    row_count = coil_image.shape[3]
    depth_pass = transform(coil_image, dft_table(depth_count, -1.0), "ctxypz,pzqk->ctxyqk").astype(
        jnp.bfloat16
    )
    row_pass = transform(depth_pass, dft_table(row_count, -1.0), "ctxypz,pyqk->ctxkqz").astype(
        jnp.bfloat16
    )
    slabs = lax.all_to_all(row_pass, "space", split_axis=3, concat_axis=2, tiled=True)
    first_count = slabs.shape[2]
    kspace = transform(slabs, dft_table(first_count, -1.0), "ctxypz,pxqk->ctkyqz")
    mask_float = sample_mask.astype(jnp.float32)[None, :, None, :, None, :]
    residual = (mask_float * (kspace - kspace_data.astype(jnp.float32))).astype(jnp.bfloat16)
    back_first = transform(residual, dft_table(first_count, 1.0), "ctxypz,pxqk->ctkyqz").astype(
        jnp.bfloat16
    )
    returned = lax.all_to_all(back_first, "space", split_axis=2, concat_axis=3, tiled=True)
    back_rows = transform(returned, dft_table(row_count, 1.0), "ctxypz,pyqk->ctxkqz").astype(
        jnp.bfloat16
    )
    back_image = transform(back_rows, dft_table(depth_count, 1.0), "ctxypz,pzqk->ctxyqk")
    back_real = back_image[:, :, :, :, 0]
    back_imaginary = back_image[:, :, :, :, 1]
    sum_real = jnp.sum(map_real * back_real + map_imaginary * back_imaginary, axis=0)
    sum_imaginary = jnp.sum(map_real * back_imaginary - map_imaginary * back_real, axis=0)
    combined_real = cosine * sum_real + sine * sum_imaginary
    combined_imaginary = cosine * sum_imaginary - sine * sum_real
    combined = jnp.stack([combined_real, combined_imaginary], axis=3)
    section = temporal_basis.astype(jnp.float32)
    return lax.psum_scatter(
        jnp.einsum(
            "txypz,tplq->lxyqz", combined, adjoint_mix(section), precision=lax.Precision.HIGHEST
        ).astype(jnp.bfloat16),
        "coil",
        scatter_dimension=0,
        tiled=True,
    ).astype(jnp.float32)


def solution(mesh):
    in_specs = (
        P("coil", "space", None, None, None),
        P(),
        P("coil", "space", None, None, None),
        P("space", None, None),
        P("coil", None, None, "space", None, None),
        P(None, "space", None),
    )
    out_specs = P("coil", "space", None, None, None)
    return jax.shard_map(shards, mesh=mesh, in_specs=in_specs, out_specs=out_specs, check_vma=False)
```

profile of v0, /device:TPU:1, one launch (start us, length us, event | category | flops | bytes accessed | tf_op | source)
XLA Modules:
  0.0 418.4 jit_solution(10272380356210166558)
XLA Ops:
  6.5 1.9 copy.65
  8.5 0.0 all-gather.2.cloned.1.call-update
  8.5 0.7 fusion.72
  9.2 0.7 slice_bitcast_fusion.6
  9.9 0.3 multiply_convert_fusion.2
  10.2 0.3 negate_convert_fusion
  10.5 0.3 multiply_convert_fusion
  10.8 3.6 slice_convert_fusion.1
  14.4 53.7 %all-gather.2.cloned.1.call-done = bf16[16,4,128,2,128]{4,2,3,1,0:T(8,128)(2,1)} async-done(((bf16[2,4,128,2,128]{4,2,3,1,0:T(8,128)(2,1)}), bf16[16,4,128,2,128]{4,2,3,1,0:T(8,128)(2,1)}) %all-gather.2.cloned.1.call-update) | async-done | bytes 4194320 | tf_op jit(solution)/shard_map/all_gather | solution.py:54
  68.1 4.9 %fusion.31 = f32[4,2,4,128,128]{4,0,3,2,1:T(4,128)S(1)} fusion(bf16[16,4,128,2,128]{4,2,3,1,0:T(8,128)(2,1)} %all-gather.2.cloned.1.call-done, bf16[16,1,4,2]{0,2,1,3:T(4,128)(2,1)S(1)} %get-tuple-element.26, bf16[16,1,4,2]{0,2,1,3:T(4,128)(2,1)S(1)} %get-tuple-element.25), kind=kOutput, calls=%fused_computation.43 | convolution fusion | flops 33555456 | bytes 6291968 | tf_op jit(solution)/shard_map/lxypz,lptq->txyqz/dot_general | solution.py:52
  73.0 0.3 copy.134
  73.2 4.6 %multiply_subtract_fusion = (f32[4,4,128,128]{3,2,1,0:T(8,128)S(1)}, f32[4,4,128,128]{3,2,1,0:T(8,128)S(1)}) fusion(f32[4,4,128,2,128]{4,2,1,0,3:T(8,128)S(1)} %bitcast.244, s32[4]{0:T(128)S(1)} %iota_add_fusion, s32[4,128,128]{2,1,0:T(8,128)S(1)} %copy-done.1), kind=kLoop, calls=%fused_computation.64 | loop fusion | flops 5242880 | bytes 4456464 | tf_op jit(solution)/shard_map/sub | solution.py:61
  77.9 3.1 subtract_convert_fusion
  81.0 6.7 %fusion.5 = bf16[4,4,4,128,2,128]{5,3,2,1,0,4:T(8,128)(2,1)} fusion(bf16[4,4,4,128,1,128]{5,3,4,2,1,0:T(8,128)(2,1)} %get-tuple-element.8, bf16[4,4,4,128,1,128]{5,3,4,2,1,0:T(8,128)(2,1)} %get-tuple-element.7, bf16[1,128,2,128]{3,1,0,2:T(8,128)(2,1)S(1)} %get-tuple-element.16, bf16[1,128,2,128]{3,1,0,2:T(8,128)(2,1)S(1)} %get-tuple-element.17), kind=kOutput, calls=%fused_computation.10 | convolution fusion | flops 2160590848 | bytes 8519680 | tf_op jit(solution)/shard_map/ctxypz,pyqk->ctxkqz/dot_general | solution.py:46
  87.7 7.4 %copy.69 = bf16[4,4,4,128,2,128]{5,2,1,0,4,3:T(4,128)(2,1)} copy(bf16[4,4,4,128,2,128]{5,3,2,1,0,4:T(8,128)(2,1)} %fusion.5) | data formatting | bytes 8388608 | tf_op jit(solution)/shard_map/convert_element_type | solution.py:73
  95.1 10.2 %all-to-all-start = ((bf16[4,4,4,128,2,128]{5,2,1,0,4,3:T(4,128)(2,1)}), bf16[4,4,4,128,2,128]{5,2,1,0,4,3:T(4,128)(2,1)}, u32[]{:S(2)}, u32[]{:S(2)}) async-start(bf16[4,4,4,128,2,128]{5,2,1,0,4,3:T(4,128)(2,1)} %copy.69), calls=%async_computation | async-start | bytes 8388608 | tf_op jit(solution)/shard_map/all_to_all | solution.py:76
  105.3 96.1 %all-to-all-done = bf16[4,4,4,128,2,128]{5,2,1,0,4,3:T(4,128)(2,1)} async-done(((bf16[4,4,4,128,2,128]{5,2,1,0,4,3:T(4,128)(2,1)}), bf16[4,4,4,128,2,128]{5,2,1,0,4,3:T(4,128)(2,1)}, u32[]{:S(2)}, u32[]{:S(2)}) %all-to-all-start) | async-done | bytes 4194336 | tf_op jit(solution)/shard_map/all_to_all | solution.py:76
  201.5 4.7 %copy.70 = bf16[4,4,4,32,4,2,128]{6,2,3,5,4,1,0:T(4,128)(2,1)S(1)} copy(bf16[4,4,4,32,4,2,128]{6,2,1,0,5,4,3:T(4,128)(2,1)} %bitcast.51) | data formatting | bytes 8388608 | tf_op jit(solution)/shard_map/all_to_all | solution.py:76
  206.2 1.4 fusion.1
  207.6 1.3 fusion.6
  208.8 5.2 %copy.75 = bf16[4,4,128,4,2,128]{5,3,1,0,4,2:T(4,128)(2,1)} copy(bf16[4,4,128,4,2,128]{5,2,3,1,0,4:T(8,128)(2,1)S(1)} %fusion.6) | data formatting | bytes 8388608 | tf_op jit(solution)/shard_map/convert_element_type | solution.py:81
  214.1 7.4 %all-to-all-start.1 = ((bf16[4,4,128,4,2,128]{5,3,1,0,4,2:T(4,128)(2,1)}), bf16[4,4,128,4,2,128]{5,3,1,0,4,2:T(4,128)(2,1)}, u32[]{:S(2)}, u32[]{:S(2)}) async-start(bf16[4,4,128,4,2,128]{5,3,1,0,4,2:T(4,128)(2,1)} %copy.75), calls=%async_computation.1 | async-start | bytes 8388608 | tf_op jit(solution)/shard_map/all_to_all | solution.py:84
  221.5 0.0 reduce-scatter.2.cloned.1.call-start
  221.6 96.1 %all-to-all-done.1 = bf16[4,4,128,4,2,128]{5,3,1,0,4,2:T(4,128)(2,1)} async-done(((bf16[4,4,128,4,2,128]{5,3,1,0,4,2:T(4,128)(2,1)}), bf16[4,4,128,4,2,128]{5,3,1,0,4,2:T(4,128)(2,1)}, u32[]{:S(2)}, u32[]{:S(2)}) %all-to-all-start.1) | async-done | bytes 4194336 | tf_op jit(solution)/shard_map/all_to_all | solution.py:84
  317.7 6.5 %copy.76 = bf16[4,4,32,4,4,2,128]{6,4,2,5,3,1,0:T(4,128)(2,1)} copy(bf16[4,4,32,4,4,2,128]{6,4,1,0,5,3,2:T(4,128)(2,1)} %bitcast.62) | data formatting | bytes 8388608 | tf_op jit(solution)/shard_map/all_to_all | solution.py:84
  324.2 7.8 %fusion.20 = f32[4,4,4,128,2,128]{5,3,4,2,1,0:T(8,128)} fusion(bf16[4,4,4,128,2,128,1]{5,3,6,4,2,1,0:T(8,128)(2,1)} %bitcast.238, bf16[1,128,2,128]{3,1,2,0:T(8,128)(2,1)S(1)} %get-tuple-element.18, bf16[1,128,2,128]{3,1,2,0:T(8,128)(2,1)S(1)} %get-tuple-element.15), kind=kOutput, calls=%fused_computation.31 | convolution fusion | flops 2150105088 | bytes 12713984 | tf_op jit(solution)/shard_map/ctxypz,pzqk->ctxyqk/dot_general | solution.py:46
  332.0 4.6 %add_reduce_fusion = (f32[4,4,128,128]{3,2,1,0:T(8,128)S(1)}, f32[4,4,128,128]{3,2,1,0:T(8,128)S(1)}) fusion(f32[4,4,4,128,2,128]{5,3,4,2,1,0:T(8,128)} %fusion.20, f32[4,4,128,128]{3,2,1,0:T(8,128)S(1)} %bitcast.243, f32[4,4,128,128]{3,2,1,0:T(8,128)S(1)} %bitcast.241), kind=kLoop, calls=%fused_computation.28 | loop fusion | flops 7864320 | bytes 12582912 | tf_op jit(solution)/shard_map/reduce_sum | solution.py:91
  336.6 9.6 %fusion.40 = (f32[4,4,128,1,128]{4,0,3,2,1:T(4,128)S(1)}, f32[4,4,128,1,128]{4,0,3,2,1:T(4,128)S(1)}) fusion(f32[4,4,128,128]{3,2,1,0:T(8,128)S(1)} %get-tuple-element.6, f32[4,4,128,128]{3,2,1,0:T(8,128)S(1)} %get-tuple-element.5, s32[4]{0:T(128)S(1)} %iota_add_fusion, s32[4,128,128]{2,1,0:T(8,128)S(1)} %copy-done.1), kind=kLoop, calls=%fused_computation.58 | loop fusion | flops 5242880 | bytes 4456464 | tf_op jit(solution)/shard_map/add | solution.py:93
  346.2 7.8 %fusion.7 = bf16[16,4,128,2,128]{4,0,2,1,3:T(8,128)(2,1)S(1)} fusion(f32[4,4,128,1,128]{4,0,3,2,1:T(4,128)S(1)} %get-tuple-element.10, f32[4,4,128,1,128]{4,0,3,2,1:T(4,128)S(1)} %get-tuple-element.9, f32[4,1,16,2]{2,0,1,3:T(4,128)S(1)} %get-tuple-element.22, f32[4,1,16,2]{2,0,1,3:T(4,128)S(1)} %get-tuple-element.21), kind=kOutput, calls=%fused_computation.12 | convolution fusion | flops 203948288 | bytes 6292480 | tf_op jit(solution)/shard_map/txypz,tplq->lxyqz/dot_general | solution.py:98
  354.0 3.1 copy.82
  357.1 51.9 %reduce-scatter.2.cloned.1.call-done = bf16[2,4,128,2,128]{4,2,3,1,0:T(8,128)(2,1)} async-done(((bf16[16,4,128,2,128]{4,2,3,1,0:T(8,128)(2,1)}), bf16[2,4,128,2,128]{4,2,3,1,0:T(8,128)(2,1)}) %reduce-scatter.2.cloned.1.call-update) | async-done | bytes 524304 | tf_op jit(solution)/shard_map/reduce_scatter | solution.py:97
  409.0 2.6 copy.83
  (18 shorter events, 0.1 us)
Async XLA Ops:
  6.5 61.6 %all-gather.2.cloned.1.call-start = ((), (), s32[]{:S(2)}) async-start(), calls=%async_computation.3 | async-start | bytes 4718592 | tf_op jit(solution)/shard_map/all_gather | solution.py:54
  68.1 5.1 %copy-start.1 = (s32[4,128,128]{2,1,0:T(8,128)S(1)}, s32[4,128,128]{2,1,0:T(8,128)}, u32[]{:S(2)}) copy-start(s32[4,128,128]{2,1,0:T(8,128)} %param.9) | copy-start | bytes 786436
  95.1 10.2 %copy-start.3 = (s32[4,4,128]{2,1,0:T(4,128)S(1)}, s32[4,4,128]{2,1,0:T(4,128)}, u32[]{:S(2)}) copy-start(s32[4,4,128]{2,1,0:T(4,128)} %param.11) | copy-start | bytes 24580
  95.1 106.3 %all-to-all-start = ((bf16[4,4,4,128,2,128]{5,2,1,0,4,3:T(4,128)(2,1)}), bf16[4,4,4,128,2,128]{5,2,1,0,4,3:T(4,128)(2,1)}, u32[]{:S(2)}, u32[]{:S(2)}) async-start(bf16[4,4,4,128,2,128]{5,2,1,0,4,3:T(4,128)(2,1)} %copy.69), calls=%async_computation | async-start | bytes 8388608 | tf_op jit(solution)/shard_map/all_to_all | solution.py:76
  201.5 4.7 %copy-start = (bf16[4,4,128,4,2,128]{5,4,3,2,1,0:T(2,128)(2,1)S(1)}, bf16[4,4,128,4,2,128]{5,4,3,2,1,0:T(2,128)(2,1)}, u32[]{:S(2)}) copy-start(bf16[4,4,128,4,2,128]{5,4,3,2,1,0:T(2,128)(2,1)} %param.10) | copy-start | bytes 12582916
  214.1 7.5 %copy-start.2 = (bf16[2,16,4]{1,2,0:T(4,128)(2,1)S(1)}, bf16[2,16,4]{1,2,0:T(4,128)(2,1)}, u32[]{:S(2)}) copy-start(bf16[2,16,4]{1,2,0:T(4,128)(2,1)} %param.7) | copy-start | bytes 772
  214.1 103.6 %all-to-all-start.1 = ((bf16[4,4,128,4,2,128]{5,3,1,0,4,2:T(4,128)(2,1)}), bf16[4,4,128,4,2,128]{5,3,1,0,4,2:T(4,128)(2,1)}, u32[]{:S(2)}, u32[]{:S(2)}) async-start(bf16[4,4,128,4,2,128]{5,3,1,0,4,2:T(4,128)(2,1)} %copy.75), calls=%async_computation.1 | async-start | bytes 8388608 | tf_op jit(solution)/shard_map/all_to_all | solution.py:84
  221.5 187.5 %reduce-scatter.2.cloned.1.call-start = ((), (), s32[]{:S(2)}) async-start(), calls=%async_computation.4 | async-start | bytes 4718592 | tf_op jit(solution)/shard_map/reduce_scatter | solution.py:97
Sparse Core Ops, SparseCore 0:
  9.1 58.9 all-gather.1
  357.2 51.7 reduce-scatter.1
where the time goes:
time: 419 us; the launch traced here: 418 us
  waiting for transfers between devices  298 us (71%)
  local copies, waits for them, and re-layouts  32.4 us (8%)
  matrix products  29.8 us (7%)
  other arithmetic  27.2 us (6%)
  starting transfers between devices  17.7 us (4%)
  between operations  13.6 us (3%)
    all_to_all x1, waiting for transfers between devices, shards(): lax.all_to_all(row_pass, 'space', split_axis=3, concat_axis=2, tiled=True)  96.1 us
    all_to_all x1, waiting for transfers between devices, shards(): lax.all_to_all(back_first, 'space', split_axis=2, concat_axis=3, tiled=True)  96.1 us
    all_gather x1, waiting for transfers between devices, shards(): lax.all_gather(spatial_coef, 'coil', axis=0, tiled=True)  53.7 us
    reduce_scatter x1, waiting for transfers between devices, shards(): lax.psum_scatter(jnp.einsum('txypz,tplq->lxyqz', combined, adjoint_mix(se...  51.9 us
    dot_general x4, matrix products, transform(): return jnp.einsum(form, volume, table, preferred_element_type=jnp.float32)  17.2 us
    all_to_all x1, starting transfers between devices, shards(): lax.all_to_all(row_pass, 'space', split_axis=3, concat_axis=2, tiled=True)  10.2 us
    add x1, other arithmetic, shards(): combined_real = cosine * sum_real + sine * sum_imaginary  9.64 us
  transfers between devices with their start and end apart: 4, of which 4 were waited for; matrix products, arithmetic and copies ran while one was open for 1% of the time, Pallas kernels for 0%

commit v1 on v0

--- a/solution.py
+++ b/solution.py
@@ -81,7 +81,12 @@
     back_first = transform(residual, dft_table(first_count, 1.0), "ctxypz,pxqk->ctkyqz").astype(
         jnp.bfloat16
     )
-    returned = lax.all_to_all(back_first, "space", split_axis=2, concat_axis=3, tiled=True)
+    returned = jnp.concatenate(
+        lax.all_to_all(
+            jnp.stack(jnp.split(back_first, lax.axis_size("space"), axis=2)), "space", 0, 0
+        ),
+        axis=3,
+    )
     back_rows = transform(returned, dft_table(row_count, 1.0), "ctxypz,pyqk->ctxkqz").astype(
         jnp.bfloat16
     )

time: 419 us -> 437 us (1.043)
  local copies, waits for them, and re-layouts: 32.4 us -> 50.4 us
    unnamed x9 -> x40, local copies, waits for them, and re-layouts: 1.95 us -> 24.3 us
    reshape x0 -> x1, local copies, waits for them, and re-layouts: none -> 6.6 us  [shards(): jnp.concatenate(lax.all_to_all(jnp.stack(jnp.split(back_first, lax.axis_s...]
    all_to_all x1 -> x0, local copies, waits for them, and re-layouts: 6.52 us -> none  [shards(): lax.all_to_all(back_first, 'space', split_axis=2, concat_axis=3, tiled=True)]
    convert_element_type x1 -> x0, local copies, waits for them, and re-layouts: 5.21 us -> none  [shards(): transform(residual, dft_table(first_count, 1.0), 'ctxypz,pxqk->ctkyqz')]
  transfers between devices with their start and end apart: 4 -> 4, of which waited for: 4 -> 4; matrix products, arithmetic and copies ran while one was open for 1% -> 2% of each run, Pallas kernels for 0% -> 0%
where the time goes in v1:
time: 437 us; the launch traced here: 436 us
  waiting for transfers between devices  297 us (68%)
  local copies, waits for them, and re-layouts  50.4 us (12%)
  matrix products  29.8 us (7%)
  other arithmetic  28.1 us (6%)
  starting transfers between devices  17.7 us (4%)
  between operations  13.6 us (3%)
    all_to_all x1, waiting for transfers between devices, shards(): lax.all_to_all(row_pass, 'space', split_axis=3, concat_axis=2, tiled=True)  96.1 us
    all_to_all x1, waiting for transfers between devices, shards(): lax.all_to_all(jnp.stack(jnp.split(back_first, lax.axis_size('space'), ax...  96.1 us
    all_gather x1, waiting for transfers between devices, shards(): lax.all_gather(spatial_coef, 'coil', axis=0, tiled=True)  52.7 us
    reduce_scatter x1, waiting for transfers between devices, shards(): lax.psum_scatter(jnp.einsum('txypz,tplq->lxyqz', combined, adjoint_mix(se...  51.9 us
    unnamed x40, local copies, waits for them, and re-layouts  24.3 us
    dot_general x4, matrix products, transform(): return jnp.einsum(form, volume, table, preferred_element_type=jnp.float32)  17.2 us
    all_to_all x1, starting transfers between devices, shards(): lax.all_to_all(row_pass, 'space', split_axis=3, concat_axis=2, tiled=True)  10.2 us
    add x1, other arithmetic, shards(): combined_real = cosine * sum_real + sine * sum_imaginary  9.64 us
  transfers between devices with their start and end apart: 4, of which 4 were waited for; matrix products, arithmetic and copies ran while one was open for 2% of the time, Pallas kernels for 0%

profile of v1, /device:TPU:1, one launch (start us, length us, event | category | flops | bytes accessed | tf_op | source)
XLA Modules:
  0.0 436.4 jit_solution(14864132081979240949)
XLA Ops:
  6.5 1.9 copy.64
  10.8 4.6 %slice_convert_fusion.1 = (f32[4,4,128,1,128]{4,3,2,1,0:T(1,128)S(1)}, f32[4,4,128,1,128]{4,3,2,1,0:T(1,128)S(1)}) fusion(bf16[4,4,128,2,128]{4,3,2,1,0:T(2,128)(2,1)} %param.8), kind=kLoop, calls=%fused_computation.65 | loop fusion | flops 524288 | bytes 3145728 | tf_op jit(solution)/shard_map/convert_element_type | solution.py:63
  15.4 52.7 %all-gather.2.cloned.1.call-done = bf16[16,4,128,2,128]{4,2,3,1,0:T(8,128)(2,1)} async-done(((bf16[2,4,128,2,128]{4,2,3,1,0:T(8,128)(2,1)}), bf16[16,4,128,2,128]{4,2,3,1,0:T(8,128)(2,1)}) %all-gather.2.cloned.1.call-update) | async-done | bytes 4194320 | tf_op jit(solution)/shard_map/all_gather | solution.py:54
  68.1 4.9 %fusion.31 = f32[4,2,4,128,128]{4,0,3,2,1:T(4,128)S(1)} fusion(bf16[16,4,128,2,128]{4,2,3,1,0:T(8,128)(2,1)} %all-gather.2.cloned.1.call-done, bf16[16,1,4,2]{0,2,1,3:T(4,128)(2,1)S(1)} %get-tuple-element.26, bf16[16,1,4,2]{0,2,1,3:T(4,128)(2,1)S(1)} %get-tuple-element.25), kind=kOutput, calls=%fused_computation.43 | convolution fusion | flops 33555456 | bytes 6291968 | tf_op jit(solution)/shard_map/lxypz,lptq->txyqz/dot_general | solution.py:52
  73.2 4.6 %multiply_subtract_fusion = (f32[4,4,128,128]{3,2,1,0:T(8,128)S(1)}, f32[4,4,128,128]{3,2,1,0:T(8,128)S(1)}) fusion(f32[4,4,128,2,128]{4,2,1,0,3:T(8,128)S(1)} %bitcast.370, s32[4]{0:T(128)S(1)} %iota_add_fusion, s32[4,128,128]{2,1,0:T(8,128)S(1)} %copy-done.1), kind=kLoop, calls=%fused_computation.64 | loop fusion | flops 5242880 | bytes 4456464 | tf_op jit(solution)/shard_map/sub | solution.py:61
  77.9 3.1 subtract_convert_fusion
  81.0 6.7 %fusion.5 = bf16[4,4,4,128,2,128]{5,3,2,1,0,4:T(8,128)(2,1)} fusion(bf16[4,4,4,128,1,128]{5,3,4,2,1,0:T(8,128)(2,1)} %get-tuple-element.8, bf16[4,4,4,128,1,128]{5,3,4,2,1,0:T(8,128)(2,1)} %get-tuple-element.7, bf16[1,128,2,128]{3,1,0,2:T(8,128)(2,1)S(1)} %get-tuple-element.16, bf16[1,128,2,128]{3,1,0,2:T(8,128)(2,1)S(1)} %get-tuple-element.17), kind=kOutput, calls=%fused_computation.10 | convolution fusion | flops 2160590848 | bytes 8519680 | tf_op jit(solution)/shard_map/ctxypz,pyqk->ctxkqz/dot_general | solution.py:46
  87.7 7.4 %copy.68 = bf16[4,4,4,128,2,128]{5,2,1,0,4,3:T(4,128)(2,1)} copy(bf16[4,4,4,128,2,128]{5,3,2,1,0,4:T(8,128)(2,1)} %fusion.5) | data formatting | bytes 8388608 | tf_op jit(solution)/shard_map/convert_element_type | solution.py:73
  95.1 10.2 %all-to-all-start = ((bf16[4,4,4,128,2,128]{5,2,1,0,4,3:T(4,128)(2,1)}), bf16[4,4,4,128,2,128]{5,2,1,0,4,3:T(4,128)(2,1)}, u32[]{:S(2)}, u32[]{:S(2)}) async-start(bf16[4,4,4,128,2,128]{5,2,1,0,4,3:T(4,128)(2,1)} %copy.68), calls=%async_computation | async-start | bytes 8388608 | tf_op jit(solution)/shard_map/all_to_all | solution.py:76
  105.3 96.1 %all-to-all-done = bf16[4,4,4,128,2,128]{5,2,1,0,4,3:T(4,128)(2,1)} async-done(((bf16[4,4,4,128,2,128]{5,2,1,0,4,3:T(4,128)(2,1)}), bf16[4,4,4,128,2,128]{5,2,1,0,4,3:T(4,128)(2,1)}, u32[]{:S(2)}, u32[]{:S(2)}) %all-to-all-start) | async-done | bytes 4194336 | tf_op jit(solution)/shard_map/all_to_all | solution.py:76
  201.5 4.7 %copy.69 = bf16[4,4,4,32,4,2,128]{6,2,3,5,4,1,0:T(4,128)(2,1)S(1)} copy(bf16[4,4,4,32,4,2,128]{6,2,1,0,5,4,3:T(4,128)(2,1)} %bitcast.51) | data formatting | bytes 8388608 | tf_op jit(solution)/shard_map/all_to_all | solution.py:76
  206.2 1.4 fusion.1
  207.6 1.3 fusion.6
  209.6 0.7 fusion.76
  214.6 0.7 fusion.69
  215.4 0.7 fusion.68
  217.5 0.7 fusion.65
  219.7 0.7 fusion.62
  221.2 0.7 fusion.60
  224.8 0.7 fusion.55
  229.8 0.7 fusion.48
  231.3 0.7 fusion.46
  232.0 7.4 %all-to-all-start.1 = ((bf16[32,4,4,4,4,2,128]{6,3,4,2,1,5,0:T(4,128)(2,1)}), bf16[32,4,4,4,4,2,128]{6,3,4,2,1,5,0:T(4,128)(2,1)}, u32[]{:S(2)}, u32[]{:S(2)}) async-start(bf16[32,4,4,4,4,2,128]{6,3,4,2,1,5,0:T(4,128)(2,1)} %fusion.46), calls=%async_computation.1 | async-start | bytes 8388608 | tf_op jit(solution)/shard_map/all_to_all | solution.py:85
  239.5 96.1 %all-to-all-done.1 = bf16[32,4,4,4,4,2,128]{6,3,4,2,1,5,0:T(4,128)(2,1)} async-done(((bf16[32,4,4,4,4,2,128]{6,3,4,2,1,5,0:T(4,128)(2,1)}), bf16[32,4,4,4,4,2,128]{6,3,4,2,1,5,0:T(4,128)(2,1)}, u32[]{:S(2)}, u32[]{:S(2)}) %all-to-all-start.1) | async-done | bytes 4194336 | tf_op jit(solution)/shard_map/all_to_all | solution.py:85
  335.6 6.6 %copy.74 = bf16[4,4,4,32,4,2,128]{6,4,3,5,2,1,0:T(4,128)(2,1)} copy(bf16[4,4,4,32,4,2,128]{6,2,4,1,0,5,3:T(4,128)(2,1)} %bitcast.94) | data formatting | bytes 8388608 | tf_op jit(solution)/shard_map/reshape | solution.py:84
  342.2 7.8 %fusion.20 = f32[4,4,4,128,2,128]{5,3,4,2,1,0:T(8,128)} fusion(bf16[4,4,4,128,2,128,1]{5,3,6,4,2,1,0:T(8,128)(2,1)} %bitcast.364, bf16[1,128,2,128]{3,1,2,0:T(8,128)(2,1)S(1)} %get-tuple-element.18, bf16[1,128,2,128]{3,1,2,0:T(8,128)(2,1)S(1)} %get-tuple-element.15), kind=kOutput, calls=%fused_computation.31 | convolution fusion | flops 2150105088 | bytes 12713984 | tf_op jit(solution)/shard_map/ctxypz,pzqk->ctxyqk/dot_general | solution.py:46
  350.0 4.6 %add_reduce_fusion = (f32[4,4,128,128]{3,2,1,0:T(8,128)S(1)}, f32[4,4,128,128]{3,2,1,0:T(8,128)S(1)}) fusion(f32[4,4,4,128,2,128]{5,3,4,2,1,0:T(8,128)} %fusion.20, f32[4,4,128,128]{3,2,1,0:T(8,128)S(1)} %bitcast.369, f32[4,4,128,128]{3,2,1,0:T(8,128)S(1)} %bitcast.367), kind=kLoop, calls=%fused_computation.28 | loop fusion | flops 7864320 | bytes 12582912 | tf_op jit(solution)/shard_map/reduce_sum | solution.py:96
  354.6 9.6 %fusion.40 = (f32[4,4,128,1,128]{4,0,3,2,1:T(4,128)S(1)}, f32[4,4,128,1,128]{4,0,3,2,1:T(4,128)S(1)}) fusion(f32[4,4,128,128]{3,2,1,0:T(8,128)S(1)} %get-tuple-element.6, f32[4,4,128,128]{3,2,1,0:T(8,128)S(1)} %get-tuple-element.5, s32[4]{0:T(128)S(1)} %iota_add_fusion, s32[4,128,128]{2,1,0:T(8,128)S(1)} %copy-done.1), kind=kLoop, calls=%fused_computation.58 | loop fusion | flops 5242880 | bytes 4456464 | tf_op jit(solution)/shard_map/add | solution.py:98
  364.2 7.8 %fusion.7 = bf16[16,4,128,2,128]{4,0,2,1,3:T(8,128)(2,1)S(1)} fusion(f32[4,4,128,1,128]{4,0,3,2,1:T(4,128)S(1)} %get-tuple-element.10, f32[4,4,128,1,128]{4,0,3,2,1:T(4,128)S(1)} %get-tuple-element.9, f32[4,1,16,2]{2,0,1,3:T(4,128)S(1)} %get-tuple-element.22, f32[4,1,16,2]{2,0,1,3:T(4,128)S(1)} %get-tuple-element.21), kind=kOutput, calls=%fused_computation.12 | convolution fusion | flops 203948288 | bytes 6292480 | tf_op jit(solution)/shard_map/txypz,tplq->lxyqz/dot_general | solution.py:103
  372.0 3.1 copy.80
  375.1 51.9 %reduce-scatter.2.cloned.1.call-done = bf16[2,4,128,2,128]{4,2,3,1,0:T(8,128)(2,1)} async-done(((bf16[16,4,128,2,128]{4,2,3,1,0:T(8,128)(2,1)}), bf16[2,4,128,2,128]{4,2,3,1,0:T(8,128)(2,1)}) %reduce-scatter.2.cloned.1.call-update) | async-done | bytes 524304 | tf_op jit(solution)/shard_map/reduce_scatter | solution.py:102
  427.0 2.6 copy.81
  (49 shorter events, 19.1 us)
Async XLA Ops:
  6.5 61.6 %all-gather.2.cloned.1.call-start = ((), (), s32[]{:S(2)}) async-start(), calls=%async_computation.3 | async-start | bytes 4718592 | tf_op jit(solution)/shard_map/all_gather | solution.py:54
  68.1 5.1 %copy-start.1 = (s32[4,128,128]{2,1,0:T(8,128)S(1)}, s32[4,128,128]{2,1,0:T(8,128)}, u32[]{:S(2)}) copy-start(s32[4,128,128]{2,1,0:T(8,128)} %param.9) | copy-start | bytes 786436
  95.1 10.2 %copy-start.3 = (s32[4,4,128]{2,1,0:T(4,128)S(1)}, s32[4,4,128]{2,1,0:T(4,128)}, u32[]{:S(2)}) copy-start(s32[4,4,128]{2,1,0:T(4,128)} %param.11) | copy-start | bytes 24580
  95.1 106.3 %all-to-all-start = ((bf16[4,4,4,128,2,128]{5,2,1,0,4,3:T(4,128)(2,1)}), bf16[4,4,4,128,2,128]{5,2,1,0,4,3:T(4,128)(2,1)}, u32[]{:S(2)}, u32[]{:S(2)}) async-start(bf16[4,4,4,128,2,128]{5,2,1,0,4,3:T(4,128)(2,1)} %copy.68), calls=%async_computation | async-start | bytes 8388608 | tf_op jit(solution)/shard_map/all_to_all | solution.py:76
  201.5 4.7 %copy-start = (bf16[4,4,128,4,2,128]{5,4,3,2,1,0:T(2,128)(2,1)S(1)}, bf16[4,4,128,4,2,128]{5,4,3,2,1,0:T(2,128)(2,1)}, u32[]{:S(2)}) copy-start(bf16[4,4,128,4,2,128]{5,4,3,2,1,0:T(2,128)(2,1)} %param.10) | copy-start | bytes 12582916
  232.0 7.5 %copy-start.2 = (bf16[2,16,4]{1,2,0:T(4,128)(2,1)S(1)}, bf16[2,16,4]{1,2,0:T(4,128)(2,1)}, u32[]{:S(2)}) copy-start(bf16[2,16,4]{1,2,0:T(4,128)(2,1)} %param.7) | copy-start | bytes 772
  232.0 103.6 %all-to-all-start.1 = ((bf16[32,4,4,4,4,2,128]{6,3,4,2,1,5,0:T(4,128)(2,1)}), bf16[32,4,4,4,4,2,128]{6,3,4,2,1,5,0:T(4,128)(2,1)}, u32[]{:S(2)}, u32[]{:S(2)}) async-start(bf16[32,4,4,4,4,2,128]{6,3,4,2,1,5,0:T(4,128)(2,1)} %fusion.46), calls=%async_computation.1 | async-start | bytes 8388608 | tf_op jit(solution)/shard_map/all_to_all | solution.py:85
  239.4 187.6 %reduce-scatter.2.cloned.1.call-start = ((), (), s32[]{:S(2)}) async-start(), calls=%async_computation.4 | async-start | bytes 4718592 | tf_op jit(solution)/shard_map/reduce_scatter | solution.py:102
Sparse Core Ops, SparseCore 0:
  9.1 58.9 all-gather.1
  375.2 51.7 reduce-scatter.1
